TPU v7x, 32 devices: a whole 2x2x4 slice. The times are simulated.
32 devices in a mesh: dp: 8 (over y, x, core), tensor: 4 (over z).
Axes of the slice: x: 2, y: 2, z: 4, core: 2. Of those that a mesh axis runs over, the one named last changes fastest.
Arguments:
- tokens: bfloat16 [8192, 2048], P(('dp', 'tensor')), may hold values from -6 to 6
- norm_attn: bfloat16 [2048], P('dp'), may hold values from 0.5 to 1.5
- w_query: bfloat16 [2048, 2048], P('dp', 'tensor'), may hold values from -0.125 to 0.125
- key_matrix: bfloat16 [2048, 1024], P('dp', 'tensor'), may hold values from -0.125 to 0.125
- value_matrix: bfloat16 [2048, 1024], P('dp', 'tensor'), may hold values from -0.125 to 0.125
- gain_query: bfloat16 [128], P('dp'), may hold values from 0.25 to 1.75
- gain_key: bfloat16 [128], P('dp'), may hold values from 0.25 to 1.75
- w_output: bfloat16 [2048, 2048], P('tensor', 'dp'), may hold values from -0.5 to 0.5
- norm_ffn: bfloat16 [2048], P('dp'), may hold values from 0.5 to 1.5
- w_gate: bfloat16 [2048, 6144], P('dp', 'tensor'), may hold values from -0.125 to 0.125
- w_up: bfloat16 [2048, 6144], P('dp', 'tensor'), may hold values from -0.125 to 0.125
- w_down: bfloat16 [6144, 2048], P('tensor', 'dp'), may hold values from -0.078125 to 0.078125
- cotangent: bfloat16 [8192, 2048], P(('dp', 'tensor')), may hold values from -6 to 6
- lengths: int32 [8], replicated, may hold values from 769 to 1024, as said below
- deal_order: int32 [8], replicated, may hold values from 0 to 7, as said below
Outputs:
- block_out: bfloat16 [8192, 2048], P(('dp', 'tensor'))
- grad_tokens: bfloat16 [8192, 2048], P(('dp', 'tensor'))
- grad_norm_attn: float32 [2048], P('dp')
- grad_query: float32 [2048, 2048], P('dp', 'tensor')
- grad_key: float32 [2048, 1024], P('dp', 'tensor')
- grad_value: float32 [2048, 1024], P('dp', 'tensor')
- grad_gain_query: float32 [128], P('dp')
- grad_gain_key: float32 [128], P('dp')
- grad_output: float32 [2048, 2048], P('tensor', 'dp')
- grad_norm_ffn: float32 [2048], P('dp')
- grad_gate: float32 [2048, 6144], P('dp', 'tensor')
- grad_up: float32 [2048, 6144], P('dp', 'tensor')
- grad_down: float32 [6144, 2048], P('tensor', 'dp')
Inputs may be any that keep to these rules, and one draw needn't show every extreme that they name: Data group g takes sequence deal_order[g]; deal_order is a permutation. `lengths`: one group's sequence fills all 1024 of its rows and another's leaves 256 - 1 rows of padding.
All inputs are finite; a program needn't handle non-finite values.
Results may differ from a plain program's by a relative error of at most 0.023.
Values may be sent and summed in bfloat16 or wider, within the bound.
No kernel may reach another device: no remote copies, remote signals or barrier semaphores. Data moves between devices by JAX's collectives and lax.ppermute only.
A program may use at most 192 MiB of HBM per device.

v0:
```python
import jax
import jax.numpy as jnp
from jax import lax
from jax.sharding import PartitionSpec as P

QUERY_HEADS = 16
KEY_VALUE_HEADS = 8
HEAD_SIZE = 128
norm_eps = 1e-06
rope_base = 1000000.0


def rms_scale(value_vectors):
    return lax.rsqrt(jnp.mean(value_vectors * value_vectors, axis=-1, keepdims=True) + norm_eps)


def rope_tables(position):
    half_dim = HEAD_SIZE // 2
    inverse_freq = rope_base ** (-2.0 * jnp.arange(half_dim, dtype=jnp.float32) / HEAD_SIZE)
    angles = position.astype(jnp.float32)[:, None] * inverse_freq[None, :]
    angles = jnp.concatenate([angles, angles], axis=1)
    return (jnp.cos(angles), jnp.sin(angles))


def rotate_half(value_vectors):
    half_dim = value_vectors.shape[-1] // 2
    return jnp.concatenate([-value_vectors[..., half_dim:], value_vectors[..., :half_dim]], axis=-1)


def rotate_back(value_vectors):
    half_dim = value_vectors.shape[-1] // 2
    return jnp.concatenate([value_vectors[..., half_dim:], -value_vectors[..., :half_dim]], axis=-1)


def group_layout(lengths, deal_order, group_id, count_of_rows):
    slots = jnp.arange(deal_order.shape[0], dtype=jnp.int32)
    seq_taken = jnp.sum(jnp.where(slots == group_id, deal_order, 0))
    seq_len = jnp.sum(jnp.where(slots == seq_taken, lengths, 0))
    row_index = jnp.arange(count_of_rows, dtype=jnp.int32)
    segment = (row_index >= seq_len).astype(jnp.int32)
    seg_start = jnp.where(segment == 0, 0, seq_len)
    return (segment, row_index - seg_start, row_index < seq_len)


def contract_rows(left, right):
    return lax.dot_general(
        left, right, (((0,), (0,)), ((), ())), preferred_element_type=jnp.float32
    )


def times_transpose(left, right):
    return lax.dot_general(
        left, right, (((1,), (1,)), ((), ())), preferred_element_type=jnp.float32
    )


def masked_scores(query_head, key_head, allowed):
    scores = jnp.einsum(
        "qgd,kd->gqk", query_head, key_head, preferred_element_type=jnp.float32
    ) * HEAD_SIZE ** (-0.5)
    return jnp.where(allowed[None], scores, -1e30)


def attend_head(query_head, key_head, value_head, allowed):
    scores = masked_scores(query_head, key_head, allowed)
    top_score = jnp.max(scores, axis=-1, keepdims=True)
    raised = jnp.exp(scores - top_score)
    summed = jnp.sum(raised, axis=-1, keepdims=True)
    attn_probs = (raised / summed).astype(jnp.bfloat16)
    context = jnp.einsum("gqk,kd->qgd", attn_probs, value_head, preferred_element_type=jnp.float32)
    return (context.astype(jnp.bfloat16), top_score[..., 0] + jnp.log(summed[..., 0]))


def attend_back(query_head, key_head, value_head, d_context_head, log_total, allowed):
    scores = masked_scores(query_head, key_head, allowed)
    attn_full = jnp.exp(scores - log_total[..., None])
    attn_probs = attn_full.astype(jnp.bfloat16)
    d_value = jnp.einsum(
        "gqk,qgd->kd", attn_probs, d_context_head, preferred_element_type=jnp.float32
    )
    d_probs = jnp.einsum(
        "qgd,kd->gqk", d_context_head, value_head, preferred_element_type=jnp.float32
    )
    row_dot = jnp.sum(attn_full * d_probs, axis=-1, keepdims=True)
    d_scores = (attn_full * (d_probs - row_dot)).astype(jnp.bfloat16)
    d_query = jnp.einsum(
        "gqk,kd->qgd", d_scores, key_head, preferred_element_type=jnp.float32
    ) * HEAD_SIZE ** (-0.5)
    d_key = jnp.einsum(
        "gqk,qgd->kd", d_scores, query_head, preferred_element_type=jnp.float32
    ) * HEAD_SIZE ** (-0.5)
    return (d_query, d_key, d_value)


def norm_back(d_unit, pre_values, pre_scale, gain_values):
    mixed_terms = gain_values * d_unit
    return pre_scale * mixed_terms - pre_values * pre_scale**3 * jnp.mean(
        mixed_terms * pre_values, axis=-1, keepdims=True
    )


def local(
    tokens,
    norm_attn,
    w_query,
    key_matrix,
    value_matrix,
    gain_query,
    gain_key,
    w_output,
    norm_ffn,
    w_gate,
    w_up,
    w_down,
    cotangent,
    lengths,
    deal_order,
):
    local_rows = tokens.shape[0]
    group_rows = local_rows * lax.axis_size("tensor")
    heads_here = QUERY_HEADS // lax.axis_size("tensor")
    key_value_local = KEY_VALUE_HEADS // lax.axis_size("tensor")
    rows_per_group = QUERY_HEADS // KEY_VALUE_HEADS
    q_width = heads_here * HEAD_SIZE
    kv_width = key_value_local * HEAD_SIZE
    segment, position, live_rows = group_layout(
        lengths, deal_order, lax.axis_index("dp"), group_rows
    )
    row_index = jnp.arange(group_rows, dtype=jnp.int32)
    allowed = (segment[:, None] == segment[None, :]) & (row_index[None, :] <= row_index[:, None])
    own_live = lax.dynamic_slice_in_dim(
        live_rows, lax.axis_index("tensor") * local_rows, local_rows
    ).astype(jnp.float32)[:, None]
    cosine_table, sine_table = rope_tables(position)
    cosine_table = cosine_table[:, None, :]
    sine_table = sine_table[:, None, :]
    full_set = (
        lax.all_gather(norm_attn, "dp", axis=0, tiled=True),
        lax.all_gather(w_query, "dp", axis=0, tiled=True),
        lax.all_gather(key_matrix, "dp", axis=0, tiled=True),
        lax.all_gather(value_matrix, "dp", axis=0, tiled=True),
        lax.all_gather(gain_query, "dp", axis=0, tiled=True),
        lax.all_gather(gain_key, "dp", axis=0, tiled=True),
        lax.all_gather(w_output, "dp", axis=1, tiled=True),
        lax.all_gather(norm_ffn, "dp", axis=0, tiled=True),
        lax.all_gather(w_gate, "dp", axis=0, tiled=True),
        lax.all_gather(w_up, "dp", axis=0, tiled=True),
        lax.all_gather(w_down, "dp", axis=1, tiled=True),
    )
    qkv_weight = jnp.concatenate((full_set[1], full_set[2], full_set[3]), axis=1)
    token_rows = tokens.astype(jnp.float32)
    scale_attn = rms_scale(token_rows)
    attention_normed_input = (token_rows * scale_attn * full_set[0].astype(jnp.float32)).astype(
        jnp.bfloat16
    )
    normed_attn_all = lax.all_gather(attention_normed_input, "tensor", axis=0, tiled=True)
    projected = jnp.dot(normed_attn_all, qkv_weight, preferred_element_type=jnp.float32)
    q_pre = projected[:, :q_width].reshape(group_rows, heads_here, HEAD_SIZE)
    key_before_norm = projected[:, q_width : q_width + kv_width].reshape(
        group_rows, key_value_local, HEAD_SIZE
    )
    value_rows = projected[:, q_width + kv_width :].astype(jnp.bfloat16)
    q_scale = rms_scale(q_pre)
    q_unit = q_pre * q_scale * full_set[4].astype(jnp.float32)
    queries = (q_unit * cosine_table + rotate_half(q_unit) * sine_table).astype(jnp.bfloat16)
    k_scale = rms_scale(key_before_norm)
    k_unit = key_before_norm * k_scale * full_set[5].astype(jnp.float32)
    key_rot = (k_unit * cosine_table + rotate_half(k_unit) * sine_table).astype(jnp.bfloat16)
    query_heads = jnp.moveaxis(
        queries.reshape(group_rows, key_value_local, rows_per_group, HEAD_SIZE), 1, 0
    )
    key_heads = jnp.moveaxis(key_rot, 1, 0)
    value_heads = jnp.moveaxis(value_rows.reshape(group_rows, key_value_local, HEAD_SIZE), 1, 0)
    context_heads, log_total = lax.map(
        lambda head_parts: attend_head(head_parts[0], head_parts[1], head_parts[2], allowed),
        (query_heads, key_heads, value_heads),
    )
    context = jnp.moveaxis(context_heads, 0, 1).reshape(group_rows, q_width)
    hidden = token_rows + lax.psum_scatter(
        jnp.dot(context, full_set[6], preferred_element_type=jnp.float32).astype(jnp.bfloat16),
        "tensor",
        scatter_dimension=0,
        tiled=True,
    ).astype(jnp.float32)
    scale_ffn = rms_scale(hidden)
    normed_ffn = (hidden * scale_ffn * full_set[7].astype(jnp.float32)).astype(jnp.bfloat16)
    normed_ffn_all = lax.all_gather(normed_ffn, "tensor", axis=0, tiled=True)
    gate_proj = jnp.dot(normed_ffn_all, full_set[8], preferred_element_type=jnp.float32)
    up_proj = jnp.dot(normed_ffn_all, full_set[9], preferred_element_type=jnp.float32)
    gate_sig = jax.nn.sigmoid(gate_proj)
    activation = (gate_proj * gate_sig * up_proj).astype(jnp.bfloat16)
    block_rows = hidden + lax.psum_scatter(
        jnp.dot(activation, full_set[10], preferred_element_type=jnp.float32).astype(jnp.bfloat16),
        "tensor",
        scatter_dimension=0,
        tiled=True,
    ).astype(jnp.float32)
    block_out = (block_rows * own_live).astype(jnp.bfloat16)
    back_set = (
        lax.all_gather(norm_attn, "dp", axis=0, tiled=True),
        lax.all_gather(w_query, "dp", axis=0, tiled=True),
        lax.all_gather(key_matrix, "dp", axis=0, tiled=True),
        lax.all_gather(value_matrix, "dp", axis=0, tiled=True),
        lax.all_gather(gain_query, "dp", axis=0, tiled=True),
        lax.all_gather(gain_key, "dp", axis=0, tiled=True),
        lax.all_gather(w_output, "dp", axis=1, tiled=True),
        lax.all_gather(norm_ffn, "dp", axis=0, tiled=True),
        lax.all_gather(w_gate, "dp", axis=0, tiled=True),
        lax.all_gather(w_up, "dp", axis=0, tiled=True),
        lax.all_gather(w_down, "dp", axis=1, tiled=True),
    )
    back_qkv = jnp.concatenate((back_set[1], back_set[2], back_set[3]), axis=1)
    d_rows = cotangent.astype(jnp.float32) * own_live
    d_branch = d_rows.astype(jnp.bfloat16)
    d_branch_all = lax.all_gather(d_branch, "tensor", axis=0, tiled=True)
    d_act = times_transpose(d_branch_all, back_set[10])
    grad_down = contract_rows(activation, d_branch_all)
    d_gate = (d_act * up_proj * gate_sig * (1.0 + gate_proj * (1.0 - gate_sig))).astype(
        jnp.bfloat16
    )
    d_up = (d_act * gate_proj * gate_sig).astype(jnp.bfloat16)
    grad_gate = contract_rows(normed_ffn_all, d_gate)
    grad_up = contract_rows(normed_ffn_all, d_up)
    d_normed_ffn = lax.psum_scatter(
        (times_transpose(d_gate, back_set[8]) + times_transpose(d_up, back_set[9])).astype(
            jnp.bfloat16
        ),
        "tensor",
        scatter_dimension=0,
        tiled=True,
    ).astype(jnp.float32)
    part_norm_ffn = jnp.sum(d_normed_ffn * hidden * scale_ffn, axis=0)
    d_hidden = d_rows + norm_back(d_normed_ffn, hidden, scale_ffn, back_set[7].astype(jnp.float32))
    d_attended = d_hidden.astype(jnp.bfloat16)
    d_attended_all = lax.all_gather(d_attended, "tensor", axis=0, tiled=True)
    d_context = times_transpose(d_attended_all, back_set[6]).astype(jnp.bfloat16)
    grad_output = contract_rows(context, d_attended_all)
    d_context_heads = jnp.moveaxis(
        d_context.reshape(group_rows, key_value_local, rows_per_group, HEAD_SIZE), 1, 0
    )
    d_query_heads, d_key_heads, d_value_heads = lax.map(
        lambda head_parts: attend_back(
            head_parts[0], head_parts[1], head_parts[2], head_parts[3], head_parts[4], allowed
        ),
        (query_heads, key_heads, value_heads, d_context_heads, log_total),
    )
    d_queries = jnp.moveaxis(d_query_heads, 0, 1).reshape(group_rows, heads_here, HEAD_SIZE)
    d_keys = jnp.moveaxis(d_key_heads, 0, 1)
    d_value = jnp.moveaxis(d_value_heads, 0, 1).reshape(group_rows, kv_width)
    du_query = d_queries * cosine_table + rotate_back(d_queries * sine_table)
    part_gain_query = jnp.sum(du_query * q_pre * q_scale, axis=(0, 1))
    d_q_pre = norm_back(du_query, q_pre, q_scale, back_set[4].astype(jnp.float32))
    du_key = d_keys * cosine_table + rotate_back(d_keys * sine_table)
    part_gain_key = jnp.sum(du_key * key_before_norm * k_scale, axis=(0, 1))
    d_k_pre = norm_back(du_key, key_before_norm, k_scale, back_set[5].astype(jnp.float32))
    d_projected = jnp.concatenate(
        (d_q_pre.reshape(group_rows, q_width), d_k_pre.reshape(group_rows, kv_width), d_value),
        axis=1,
    ).astype(jnp.bfloat16)
    grad_qkv = contract_rows(normed_attn_all, d_projected)
    grad_query = grad_qkv[:, :q_width]
    grad_key = grad_qkv[:, q_width : q_width + kv_width]
    grad_value = grad_qkv[:, q_width + kv_width :]
    d_normed_attn = lax.psum_scatter(
        times_transpose(d_projected, back_qkv).astype(jnp.bfloat16),
        "tensor",
        scatter_dimension=0,
        tiled=True,
    ).astype(jnp.float32)
    part_norm_attn = jnp.sum(d_normed_attn * token_rows * scale_attn, axis=0)
    d_tokens = d_hidden + norm_back(
        d_normed_attn, token_rows, scale_attn, back_set[0].astype(jnp.float32)
    )
    gain_parts = lax.psum((part_norm_attn, part_norm_ffn, part_gain_query, part_gain_key), "tensor")
    shards = tuple(
        (
            lax.psum_scatter(
                gain_parts[0].astype(jnp.bfloat16), "dp", scatter_dimension=0, tiled=True
            ).astype(jnp.float32),
            lax.psum_scatter(
                grad_query.astype(jnp.bfloat16), "dp", scatter_dimension=0, tiled=True
            ).astype(jnp.float32),
            lax.psum_scatter(
                grad_key.astype(jnp.bfloat16), "dp", scatter_dimension=0, tiled=True
            ).astype(jnp.float32),
            lax.psum_scatter(
                grad_value.astype(jnp.bfloat16), "dp", scatter_dimension=0, tiled=True
            ).astype(jnp.float32),
            lax.psum_scatter(
                gain_parts[2].astype(jnp.bfloat16), "dp", scatter_dimension=0, tiled=True
            ).astype(jnp.float32),
            lax.psum_scatter(
                gain_parts[3].astype(jnp.bfloat16), "dp", scatter_dimension=0, tiled=True
            ).astype(jnp.float32),
            lax.psum_scatter(
                grad_output.astype(jnp.bfloat16), "dp", scatter_dimension=1, tiled=True
            ).astype(jnp.float32),
            lax.psum_scatter(
                gain_parts[1].astype(jnp.bfloat16), "dp", scatter_dimension=0, tiled=True
            ).astype(jnp.float32),
            lax.psum_scatter(
                grad_gate.astype(jnp.bfloat16), "dp", scatter_dimension=0, tiled=True
            ).astype(jnp.float32),
            lax.psum_scatter(
                grad_up.astype(jnp.bfloat16), "dp", scatter_dimension=0, tiled=True
            ).astype(jnp.float32),
            lax.psum_scatter(
                grad_down.astype(jnp.bfloat16), "dp", scatter_dimension=1, tiled=True
            ).astype(jnp.float32),
        )
    )
    return (block_out, d_tokens.astype(jnp.bfloat16)) + shards


def solution(mesh):
    return jax.shard_map(
        local,
        mesh=mesh,
        in_specs=(
            P(("dp", "tensor"), None),
            P("dp"),
            P("dp", "tensor"),
            P("dp", "tensor"),
            P("dp", "tensor"),
            P("dp"),
            P("dp"),
            P("tensor", "dp"),
            P("dp"),
            P("dp", "tensor"),
            P("dp", "tensor"),
            P("tensor", "dp"),
            P(("dp", "tensor"), None),
            P(),
            P(),
        ),
        out_specs=(
            P(("dp", "tensor"), None),
            P(("dp", "tensor"), None),
            P("dp"),
            P("dp", "tensor"),
            P("dp", "tensor"),
            P("dp", "tensor"),
            P("dp"),
            P("dp"),
            P("tensor", "dp"),
            P("dp"),
            P("dp", "tensor"),
            P("dp", "tensor"),
            P("tensor", "dp"),
        ),
        check_vma=False,
    )
```

profile of v0, /device:TPU:0, one launch (start us, length us, event | category | flops | bytes accessed | tf_op | source)
XLA Modules:
  0.0 1377.7 jit_solution(12239359164739884811)
XLA Ops:
  31.5 13.4 all-reduce.8
  51.2 14.9 %all-gather.18.cloned.1.call-done = bf16[2048,256]{1,0:T(8,128)(2,1)} async-done(((bf16[256,256]{1,0:T(8,128)(2,1)}), bf16[2048,256]{1,0:T(8,128)(2,1)}) %all-gather.18.cloned.1.call-update) | async-done | bytes 1048592 | tf_op jit(solution)/shard_map/all_gather | solution.py:140
  68.4 23.1 %all-gather.20.cloned.1.call-done = bf16[2048,256]{1,0:T(8,128)(2,1)} async-done(((bf16[256,256]{1,0:T(8,128)(2,1)}), bf16[2048,256]{1,0:T(8,128)(2,1)}) %all-gather.20.cloned.1.call-update) | async-done | bytes 1048592 | tf_op jit(solution)/shard_map/all_gather | solution.py:141
  93.9 80.5 %all-gather.14.cloned.1.call-done = bf16[1024,2048]{1,0:T(8,128)(2,1)} async-done(((bf16[256,2048]{1,0:T(8,128)(2,1)}), bf16[1024,2048]{1,0:T(8,128)(2,1)}) %all-gather.14.cloned.1.call-update) | async-done | bytes 4194320 | tf_op jit(solution)/shard_map/all_gather | solution.py:156
  206.1 16.8 %while.28 = (s32[]{:T(128)}, bf16[2,1024,2,128]{1,3,2,0:T(8,128)(2,1)}, f32[2,2,1024]{2,1,0:T(2,128)S(1)}, bf16[2,1024,128]{1,2,0:T(8,128)(2,1)S(1)}, bf16[2,102...) while((s32[]{:T(128)}, ...), condition=%wide.region_8.9_spmd.clone, body=%wide.region_5.8_spmd.clone.sunk | while | flops 1102313472 | bytes 31004760 | solution.py:174
  240.0 65.8 %reduce-scatter.12.cloned.1.call-done = bf16[256,2048]{1,0:T(8,128)(2,1)} async-done(((bf16[1024,2048]{1,0:T(8,128)(2,1)}), bf16[256,2048]{1,0:T(8,128)(2,1)}) %reduce-scatter.12.cloned.1.call-update) | async-done | bytes 1048592 | tf_op jit(solution)/shard_map/reduce_scatter | solution.py:179
  313.6 40.3 %all-gather.26.cloned.1.call-done = bf16[2048,1536]{1,0:T(8,128)(2,1)} async-done(((bf16[256,1536]{1,0:T(8,128)(2,1)}), bf16[2048,1536]{1,0:T(8,128)(2,1)}) %all-gather.26.cloned.1.call-update) | async-done | bytes 6291472 | tf_op jit(solution)/shard_map/all_gather | solution.py:146
  353.9 83.0 %all-gather.24.cloned.1.call-done = bf16[1024,2048]{1,0:T(8,128)(2,1)} async-done(((bf16[256,2048]{1,0:T(8,128)(2,1)}), bf16[1024,2048]{1,0:T(8,128)(2,1)}) %all-gather.24.cloned.1.call-update) | async-done | bytes 4194320 | tf_op jit(solution)/shard_map/all_gather | solution.py:187
  448.8 34.2 %all-gather.28.cloned.1.call-done = bf16[2048,1536]{1,0:T(8,128)(2,1)} async-done(((bf16[256,1536]{1,0:T(8,128)(2,1)}), bf16[2048,1536]{1,0:T(8,128)(2,1)}) %all-gather.28.cloned.1.call-update) | async-done | bytes 6291472 | tf_op jit(solution)/shard_map/all_gather | solution.py:147
  494.7 71.2 %all-gather.32.cloned.1.call-done = bf16[1024,2048]{1,0:T(8,128)(2,1)} async-done(((bf16[256,2048]{1,0:T(8,128)(2,1)}), bf16[1024,2048]{1,0:T(8,128)(2,1)}) %all-gather.32.cloned.1.call-update) | async-done | bytes 4194320 | tf_op jit(solution)/shard_map/all_gather | solution.py:215
  565.9 47.3 %all-gather.30.cloned.1.call-done = bf16[1536,2048]{1,0:T(8,128)(2,1)} async-done(((bf16[1536,256]{1,0:T(8,128)(2,1)}), bf16[1536,2048]{1,0:T(8,128)(2,1)}) %all-gather.30.cloned.1.call-update) | async-done | bytes 6291472 | tf_op jit(solution)/shard_map/all_gather | solution.py:148
  613.2 16.5 %multiply_convert_fusion = (bf16[1024,1536]{1,0:T(8,128)(2,1)}, bf16[1024,1536]{1,0:T(8,128)(2,1)S(1)}, bf16[1024,1536]{1,0:T(8,128)(2,1)}) fusion(f32[1024,1536]{1,0:T(8,128)} %fusion.113, f32[1024,1536]{1,0:T(8,128)} %fusion.114, bf16[1024,2048]{1,0:T(8,128)(2,1)} %all-gather.32.cloned.1.call-done, bf16[1536,2048]{1,0:T(8,128)(2,1)} %all-gather.30.cloned.1.call-done), kind=kOutput, calls=%fused_computation.75 | convolution fusion | flops 6467616768 | bytes 32505856 | tf_op jit(solution)/shard_map/dot_general | solution.py:52
  661.4 65.7 %reduce-scatter.16.cloned.1.call-done = bf16[256,2048]{1,0:T(8,128)(2,1)} async-done(((bf16[1024,2048]{1,0:T(8,128)(2,1)}), bf16[256,2048]{1,0:T(8,128)(2,1)}) %reduce-scatter.16.cloned.1.call-update) | async-done | bytes 1048592 | tf_op jit(solution)/shard_map/reduce_scatter | solution.py:224
  729.6 77.1 %reduce-scatter.14.cloned.1.call-done = bf16[256,2048]{1,0:T(8,128)(2,1)} async-done(((bf16[1024,2048]{1,0:T(8,128)(2,1)}), bf16[256,2048]{1,0:T(8,128)(2,1)}) %reduce-scatter.14.cloned.1.call-update) | async-done | bytes 1048592 | tf_op jit(solution)/shard_map/reduce_scatter | solution.py:192
  850.0 43.1 %all-gather.34.cloned.1.call-done = bf16[1024,2048]{1,0:T(8,128)(2,1)} async-done(((bf16[256,2048]{1,0:T(8,128)(2,1)}), bf16[1024,2048]{1,0:T(8,128)(2,1)}) %all-gather.34.cloned.1.call-update) | async-done | bytes 4194320 | tf_op jit(solution)/shard_map/all_gather | solution.py:235
  901.8 27.5 %while.29 = (s32[]{:T(128)}, f32[2,1024,2,128]{1,3,2,0:T(8,128)}, f32[2,1024,128]{2,1,0:T(8,128)}, bf16[2,1024,128]{2,1,0:T(8,128)(2,1)}, bf16[2,1024,128]{2,1,0...) while((s32[]{:T(128)}, f32[2,1024,2,128]{1,3,2,0:T(8,128)}, ...), condition=%wide.region_16.17_spmd.clone, body=%wide.region_14.16_spmd.clone.sunk | while | flops 2719348736 | bytes 101516552 | solution.py:241
  974.8 47.3 %reduce-scatter.30.cloned.1.call-done = bf16[256,1536]{1,0:T(8,128)(2,1)} async-done(((bf16[2048,1536]{1,0:T(8,128)(2,1)}), bf16[256,1536]{1,0:T(8,128)(2,1)}) %reduce-scatter.30.cloned.1.call-update) | async-done | bytes 786448 | tf_op jit(solution)/shard_map/reduce_scatter | solution.py:304
  1024.6 62.9 %reduce-scatter.32.cloned.1.call-done = bf16[1536,256]{1,0:T(8,128)(2,1)} async-done(((bf16[1536,2048]{1,0:T(8,128)(2,1)}), bf16[1536,256]{1,0:T(8,128)(2,1)}) %reduce-scatter.32.cloned.1.call-update) | async-done | bytes 786448 | tf_op jit(solution)/shard_map/reduce_scatter | solution.py:307
  1089.9 36.7 %reduce-scatter.22.cloned.1.call-done = bf16[256,256]{1,0:T(8,128)(2,1)} async-done(((bf16[2048,256]{1,0:T(8,128)(2,1)}), bf16[256,256]{1,0:T(8,128)(2,1)}) %reduce-scatter.22.cloned.1.call-update) | async-done | bytes 131088 | tf_op jit(solution)/shard_map/reduce_scatter | solution.py:283
  1128.2 37.6 %reduce-scatter.24.cloned.1.call-done = bf16[256,256]{1,0:T(8,128)(2,1)} async-done(((bf16[2048,256]{1,0:T(8,128)(2,1)}), bf16[256,256]{1,0:T(8,128)(2,1)}) %reduce-scatter.24.cloned.1.call-update) | async-done | bytes 131088 | tf_op jit(solution)/shard_map/reduce_scatter | solution.py:286
  1167.4 42.8 %reduce-scatter.26.cloned.1.call-done = bf16[512,256]{1,0:T(8,128)(2,1)} async-done(((bf16[512,2048]{1,0:T(8,128)(2,1)}), bf16[512,256]{1,0:T(8,128)(2,1)}) %reduce-scatter.26.cloned.1.call-update) | async-done | bytes 262160 | tf_op jit(solution)/shard_map/reduce_scatter | solution.py:295
  1211.9 43.1 %reduce-scatter.20.cloned.1.call-done = bf16[256,512]{1,0:T(8,128)(2,1)} async-done(((bf16[2048,512]{1,0:T(8,128)(2,1)}), bf16[256,512]{1,0:T(8,128)(2,1)}) %reduce-scatter.20.cloned.1.call-update) | async-done | bytes 262160 | tf_op jit(solution)/shard_map/reduce_scatter | solution.py:280
  1256.9 77.3 %reduce-scatter.18.cloned.1.call-done = bf16[256,2048]{1,0:T(8,128)(2,1)} async-done(((bf16[1024,2048]{1,0:T(8,128)(2,1)}), bf16[256,2048]{1,0:T(8,128)(2,1)}) %reduce-scatter.18.cloned.1.call-update) | async-done | bytes 1048592 | tf_op jit(solution)/shard_map/reduce_scatter | solution.py:264
  1336.0 18.2 %all-reduce.6 = (bf16[2048]{0:T(1024)(128)(2,1)S(1)}, bf16[128]{0:T(256)(128)(2,1)S(1)}, bf16[128]{0:T(256)(128)(2,1)S(1)}, bf16[2048]{0:T(1024)(128)(2,1)S(1)}) all-reduce(f32[2048]{0:T(1024)S(1)} %get-tuple-element.175, f32[128]{0:T(128)S(1)} %bitcast_reduce_fusion, ...), channel_id=1, replica_groups=mesh['dp'=8,'tensor'=4] {'tensor'}, use_global_device_ids=true, to_apply=%region_22.23 | all-reduce | flops 4352 | bytes 26112 | tf_op jit(solution)/shard_map/psum | solution.py:274
  (303 shorter events, 318.0 us)
Async XLA Ops:
  7.2 40.8 %all-gather.16.cloned.1.call-start = ((), (), s32[]{:S(2)}) async-start(), calls=%async_computation.12 | async-start | bytes 2359296 | tf_op jit(solution)/shard_map/all_gather | solution.py:139
  8.0 58.1 %all-gather.18.cloned.1.call-start = ((), (), s32[]{:S(2)}) async-start(), calls=%async_computation.13 | async-start | bytes 1179648 | tf_op jit(solution)/shard_map/all_gather | solution.py:140
  8.7 82.8 %all-gather.20.cloned.1.call-start = ((), (), s32[]{:S(2)}) async-start(), calls=%async_computation.14 | async-start | bytes 1179648 | tf_op jit(solution)/shard_map/all_gather | solution.py:141
  9.5 164.9 %all-gather.14.cloned.1.call-start = ((), (), s32[]{:S(2)}) async-start(), calls=%async_computation.11 | async-start | bytes 5242880 | tf_op jit(solution)/shard_map/all_gather | solution.py:156
  25.7 197.3 %all-gather.22.cloned.1.call-start = ((), (), s32[]{:S(2)}) async-start(), calls=%async_computation.15 | async-start | bytes 2359296 | tf_op jit(solution)/shard_map/all_gather | solution.py:144
  26.3 279.5 %reduce-scatter.12.cloned.1.call-start = ((), (), s32[]{:S(2)}) async-start(), calls=%async_computation.16 | async-start | bytes 5242880 | tf_op jit(solution)/shard_map/reduce_scatter | solution.py:179
  230.3 123.6 %all-gather.26.cloned.1.call-start = ((), (), s32[]{:S(2)}) async-start(), calls=%async_computation.18 | async-start | bytes 7077888 | tf_op jit(solution)/shard_map/all_gather | solution.py:146
  231.0 205.9 %all-gather.24.cloned.1.call-start = ((), (), s32[]{:S(2)}) async-start(), calls=%async_computation.17 | async-start | bytes 5242880 | tf_op jit(solution)/shard_map/all_gather | solution.py:187
  310.0 173.0 %all-gather.28.cloned.1.call-start = ((), (), s32[]{:S(2)}) async-start(), calls=%async_computation.19 | async-start | bytes 7077888 | tf_op jit(solution)/shard_map/all_gather | solution.py:147
  310.8 255.1 %all-gather.32.cloned.1.call-start = ((), (), s32[]{:S(2)}) async-start(), calls=%async_computation.22 | async-start | bytes 5242880 | tf_op jit(solution)/shard_map/all_gather | solution.py:215
  312.8 300.3 %all-gather.30.cloned.1.call-start = ((), (), s32[]{:S(2)}) async-start(), calls=%async_computation.20 | async-start | bytes 7077888 | tf_op jit(solution)/shard_map/all_gather | solution.py:148
  313.6 413.5 %reduce-scatter.16.cloned.1.call-start = ((), (), s32[]{:S(2)}) async-start(), calls=%async_computation.23 | async-start | bytes 5242880 | tf_op jit(solution)/shard_map/reduce_scatter | solution.py:224
  650.2 156.5 %reduce-scatter.14.cloned.1.call-start = ((), (), s32[]{:S(2)}) async-start(), calls=%async_computation.21 | async-start | bytes 5242880 | tf_op jit(solution)/shard_map/reduce_scatter | solution.py:192
  661.3 231.8 %all-gather.34.cloned.1.call-start = ((), (), s32[]{:S(2)}) async-start(), calls=%async_computation.24 | async-start | bytes 5242880 | tf_op jit(solution)/shard_map/all_gather | solution.py:235
  811.8 160.4 %reduce-scatter.28.cloned.1.call-start = ((), (), s32[]{:S(2)}) async-start(), calls=%async_computation.30 | async-start | bytes 7077888 | tf_op jit(solution)/shard_map/reduce_scatter | solution.py:301
  823.3 198.8 %reduce-scatter.30.cloned.1.call-start = ((), (), s32[]{:S(2)}) async-start(), calls=%async_computation.31 | async-start | bytes 7077888 | tf_op jit(solution)/shard_map/reduce_scatter | solution.py:304
  835.3 252.2 %reduce-scatter.32.cloned.1.call-start = ((), (), s32[]{:S(2)}) async-start(), calls=%async_computation.32 | async-start | bytes 7077888 | tf_op jit(solution)/shard_map/reduce_scatter | solution.py:307
  850.0 276.6 %reduce-scatter.22.cloned.1.call-start = ((), (), s32[]{:S(2)}) async-start(), calls=%async_computation.27 | async-start | bytes 1179648 | tf_op jit(solution)/shard_map/reduce_scatter | solution.py:283
  952.1 213.6 %reduce-scatter.24.cloned.1.call-start = ((), (), s32[]{:S(2)}) async-start(), calls=%async_computation.28 | async-start | bytes 1179648 | tf_op jit(solution)/shard_map/reduce_scatter | solution.py:286
  952.9 257.2 %reduce-scatter.26.cloned.1.call-start = ((), (), s32[]{:S(2)}) async-start(), calls=%async_computation.29 | async-start | bytes 2359296 | tf_op jit(solution)/shard_map/reduce_scatter | solution.py:295
  959.1 295.9 %reduce-scatter.20.cloned.1.call-start = ((), (), s32[]{:S(2)}) async-start(), calls=%async_computation.26 | async-start | bytes 2359296 | tf_op jit(solution)/shard_map/reduce_scatter | solution.py:280
  962.3 371.8 %reduce-scatter.18.cloned.1.call-start = ((), (), s32[]{:S(2)}) async-start(), calls=%async_computation.25 | async-start | bytes 5242880 | tf_op jit(solution)/shard_map/reduce_scatter | solution.py:264
  974.8 393.0 %copy-start.17 = (f32[256,2048]{1,0:T(8,128)S(1)}, f32[256,2048]{1,0:T(8,128)}, u32[]{:S(2)}) copy-start(f32[256,2048]{1,0:T(8,128)} %get-tuple-element.223) | copy-start | bytes 6291460
  974.8 393.0 %copy-start.47 = (f32[256]{0:T(256)S(1)}, f32[256]{0:T(256)}, u32[]{:S(2)}) copy-start(f32[256]{0:T(256)} %get-tuple-element.252) | copy-start | bytes 3076
  (61 other events, 2283.4 us)
Sparse Core Ops, SparseCore 0:
  10.0 30.6 all-gather.15
  42.5 23.5 all-gather.17
  68.0 23.4 all-gather.19
  93.5 80.7 all-gather.13
  176.0 26.7 all-gather.21
  230.4 75.3 reduce-scatter.11
  307.8 46.0 all-gather.25
  356.1 80.7 all-gather.23
  438.9 44.0 all-gather.27
  485.1 80.7 all-gather.31
  567.9 45.1 all-gather.29
  650.3 76.7 reduce-scatter.15
  729.4 77.2 reduce-scatter.13
  811.9 81.2 all-gather.33
  896.8 60.2 reduce-scatter.27
  960.3 61.7 reduce-scatter.29
  1025.7 61.7 reduce-scatter.31
  1090.5 36.0 reduce-scatter.21
  1129.7 35.9 reduce-scatter.23
  1168.9 41.2 reduce-scatter.25
  1213.8 41.2 reduce-scatter.19
  1257.4 76.7 reduce-scatter.17
where the time goes:
time: 1390 us; the launch traced here: 1380 us
  waiting for transfers between devices  999 us (72%)
  matrix products  176 us (13%)
  other arithmetic  76.1 us (5%)
  blocking collectives  63.1 us (5%)
  local copies, waits for them, and re-layouts  44.2 us (3%)
  between operations  17.3 us (1%)
    all_gather x1, waiting for transfers between devices, local(): normed_ffn_all = lax.all_gather(normed_ffn, 'tensor', axis=0, tiled=True)  83 us
    all_gather x1, waiting for transfers between devices, local(): lax.all_gather(attention_normed_input, 'tensor', axis=0, tiled=True)  80.5 us
    reduce_scatter x1, waiting for transfers between devices, local(): lax.psum_scatter(times_transpose(d_projected, back_qkv).astype(jnp.bfloat...  77.3 us
    reduce_scatter x1, waiting for transfers between devices, local(): lax.psum_scatter(jnp.dot(activation, full_set[10], preferred_element_type...  77.1 us
    all_gather x1, waiting for transfers between devices, local(): d_branch_all = lax.all_gather(d_branch, 'tensor', axis=0, tiled=True)  71.2 us
    reduce_scatter x1, waiting for transfers between devices, local(): lax.psum_scatter(jnp.dot(context, full_set[6], preferred_element_type=jnp...  65.8 us
    reduce_scatter x1, waiting for transfers between devices, local(): lax.psum_scatter((times_transpose(d_gate, back_set[8]) + times_transpose(...  65.7 us
    reduce_scatter x1, waiting for transfers between devices, local(): lax.psum_scatter(grad_down.astype(jnp.bfloat16), 'dp', scatter_dimension=...  62.9 us
  transfers between devices with their start and end apart: 22, of which 19 were waited for; matrix products, arithmetic and copies ran while one was open for 17% of the time, Pallas kernels for 0%

commit v1 on v0

--- a/solution.py
+++ b/solution.py
@@ -212,7 +212,14 @@
     back_qkv = jnp.concatenate((back_set[1], back_set[2], back_set[3]), axis=1)
     d_rows = cotangent.astype(jnp.float32) * own_live
     d_branch = d_rows.astype(jnp.bfloat16)
-    d_branch_all = lax.all_gather(d_branch, "tensor", axis=0, tiled=True)
+    ring = [d_branch]
+    for hop in range(3):
+        ring.append(lax.ppermute(ring[-1], "tensor", [(dev, (dev + 1) % 4) for dev in range(4)]))
+    d_branch_all = jnp.roll(
+        jnp.concatenate(ring[::-1], axis=0),
+        (lax.axis_index("tensor") + 1) * ring[0].shape[0],
+        axis=0,
+    )
     d_act = times_transpose(d_branch_all, back_set[10])
     grad_down = contract_rows(activation, d_branch_all)
     d_gate = (d_act * up_proj * gate_sig * (1.0 + gate_proj * (1.0 - gate_sig))).astype(

time: 1390 us -> 1330 us (0.957)
  waiting for transfers between devices: 999 us -> 924 us
    ppermute x0 -> x3, waiting for transfers between devices: none -> 101 us  [local(): lax.ppermute(ring[-1], 'tensor', [(dev, (dev + 1) % 4) for dev in range(4)])]
    all_gather x1 -> x0, waiting for transfers between devices: 71.2 us -> none  [local(): d_branch_all = lax.all_gather(d_branch, 'tensor', axis=0, tiled=True)]
    reduce_scatter x1, waiting for transfers between devices: 62.9 us -> 0.02 us  [local(): lax.psum_scatter(grad_down.astype(jnp.bfloat16), 'dp', scatter_dimension=...]
    all_gather x1, waiting for transfers between devices: 83 us -> 29.7 us  [local(): normed_ffn_all = lax.all_gather(normed_ffn, 'tensor', axis=0, tiled=True)]
    reduce_scatter x1, waiting for transfers between devices: 0.02 us -> 47.5 us  [local(): lax.psum_scatter(grad_gate.astype(jnp.bfloat16), 'dp', scatter_dimension=...]
    all_gather x1, waiting for transfers between devices: 40.3 us -> 0.01 us  [local(): lax.all_gather(w_gate, 'dp', axis=0, tiled=True)]
    reduce_scatter x1, waiting for transfers between devices: 47.3 us -> 62.9 us  [local(): lax.psum_scatter(grad_up.astype(jnp.bfloat16), 'dp', scatter_dimension=0,...]
    unnamed x113 -> x121, local copies, waits for them, and re-layouts: 16.9 us -> 29.5 us
  transfers between devices with their start and end apart: 22 -> 24, of which waited for: 19 -> 20; matrix products, arithmetic and copies ran while one was open for 17% -> 18% of each run, Pallas kernels for 0% -> 0%
where the time goes in v1:
time: 1330 us; the launch traced here: 1320 us
  waiting for transfers between devices  924 us (69%)
  matrix products  176 us (13%)
  other arithmetic  77.5 us (6%)
  blocking collectives  63 us (5%)
  local copies, waits for them, and re-layouts  56.7 us (4%)
  between operations  17.3 us (1%)
    ppermute x3, waiting for transfers between devices, local(): lax.ppermute(ring[-1], 'tensor', [(dev, (dev + 1) % 4) for dev in range(4)])  101 us
    all_gather x1, waiting for transfers between devices, local(): lax.all_gather(attention_normed_input, 'tensor', axis=0, tiled=True)  80.4 us
    reduce_scatter x1, waiting for transfers between devices, local(): lax.psum_scatter(times_transpose(d_projected, back_qkv).astype(jnp.bfloat...  77.3 us
    reduce_scatter x1, waiting for transfers between devices, local(): lax.psum_scatter(jnp.dot(activation, full_set[10], preferred_element_type...  76.6 us
    reduce_scatter x1, waiting for transfers between devices, local(): lax.psum_scatter(jnp.dot(context, full_set[6], preferred_element_type=jnp...  65.8 us
    reduce_scatter x1, waiting for transfers between devices, local(): lax.psum_scatter((times_transpose(d_gate, back_set[8]) + times_transpose(...  65.7 us
    reduce_scatter x1, waiting for transfers between devices, local(): lax.psum_scatter(grad_up.astype(jnp.bfloat16), 'dp', scatter_dimension=0,...  62.9 us
    dot_general x5, matrix products, times_transpose(): lax.dot_general(left, right, (((1,), (1,)), ((), ())), preferred_element_...  51.4 us
  transfers between devices with their start and end apart: 24, of which 20 were waited for; matrix products, arithmetic and copies ran while one was open for 18% of the time, Pallas kernels for 0%

profile of v1, /device:TPU:0, one launch (start us, length us, event | category | flops | bytes accessed | tf_op | source)
XLA Modules:
  0.0 1317.7 jit_solution(9998473519830774780)
XLA Ops:
  50.9 15.2 %all-gather.17.cloned.1.call-done = bf16[2048,256]{1,0:T(8,128)(2,1)} async-done(((bf16[256,256]{1,0:T(8,128)(2,1)}), bf16[2048,256]{1,0:T(8,128)(2,1)}) %all-gather.17.cloned.1.call-update) | async-done | bytes 1048592 | tf_op jit(solution)/shard_map/all_gather | solution.py:140
  68.5 23.1 %all-gather.19.cloned.1.call-done = bf16[2048,256]{1,0:T(8,128)(2,1)} async-done(((bf16[256,256]{1,0:T(8,128)(2,1)}), bf16[2048,256]{1,0:T(8,128)(2,1)}) %all-gather.19.cloned.1.call-update) | async-done | bytes 1048592 | tf_op jit(solution)/shard_map/all_gather | solution.py:141
  93.9 80.4 %all-gather.13.cloned.1.call-done = bf16[1024,2048]{1,0:T(8,128)(2,1)} async-done(((bf16[256,2048]{1,0:T(8,128)(2,1)}), bf16[1024,2048]{1,0:T(8,128)(2,1)}) %all-gather.13.cloned.1.call-update) | async-done | bytes 4194320 | tf_op jit(solution)/shard_map/all_gather | solution.py:156
  206.2 16.8 %while.28 = (s32[]{:T(128)}, bf16[2,1024,2,128]{1,3,2,0:T(8,128)(2,1)}, f32[2,2,1024]{2,1,0:T(2,128)S(1)}, bf16[2,1024,128]{1,2,0:T(8,128)(2,1)S(1)}, bf16[2,102...) while((s32[]{:T(128)}, ...), condition=%wide.region_8.9_spmd.clone, body=%wide.region_5.8_spmd.clone.sunk | while | flops 1102313472 | bytes 31004760 | solution.py:174
  240.0 65.8 %reduce-scatter.12.cloned.1.call-done = bf16[256,2048]{1,0:T(8,128)(2,1)} async-done(((bf16[1024,2048]{1,0:T(8,128)(2,1)}), bf16[256,2048]{1,0:T(8,128)(2,1)}) %reduce-scatter.12.cloned.1.call-update) | async-done | bytes 1048592 | tf_op jit(solution)/shard_map/reduce_scatter | solution.py:179
  313.8 25.2 %collective-permute-done = bf16[256,2048]{1,0:T(8,128)(2,1)S(1)} collective-permute-done((bf16[256,2048]{1,0:T(8,128)(2,1)S(1)}, bf16[256,2048]{1,0:T(8,128)(2,1)S(1)}, u32[]{:S(2)}, u32[]{:S(2)}) %collective-permute-start) | collective-permute-done | bytes 1048608 | tf_op jit(solution)/shard_map/ppermute | solution.py:217
  340.0 26.0 %collective-permute-done.1 = bf16[256,2048]{1,0:T(8,128)(2,1)} collective-permute-done((bf16[256,2048]{1,0:T(8,128)(2,1)S(1)}, bf16[256,2048]{1,0:T(8,128)(2,1)}, u32[]{:S(2)}, u32[]{:S(2)}) %collective-permute-start.1) | collective-permute-done | bytes 1048608 | tf_op jit(solution)/shard_map/ppermute | solution.py:217
  366.0 49.5 %collective-permute-done.2 = bf16[256,2048]{1,0:T(8,128)(2,1)} collective-permute-done((bf16[256,2048]{1,0:T(8,128)(2,1)}, bf16[256,2048]{1,0:T(8,128)(2,1)}, u32[]{:S(2)}, u32[]{:S(2)}) %collective-permute-start.2) | collective-permute-done | bytes 1048608 | tf_op jit(solution)/shard_map/ppermute | solution.py:217
  429.5 29.7 %all-gather.23.cloned.1.call-done = bf16[1024,2048]{1,0:T(8,128)(2,1)} async-done(((bf16[256,2048]{1,0:T(8,128)(2,1)}), bf16[1024,2048]{1,0:T(8,128)(2,1)}) %all-gather.23.cloned.1.call-update) | async-done | bytes 4194320 | tf_op jit(solution)/shard_map/all_gather | solution.py:187
  471.0 34.1 %all-gather.27.cloned.1.call-done = bf16[2048,1536]{1,0:T(8,128)(2,1)} async-done(((bf16[256,1536]{1,0:T(8,128)(2,1)}), bf16[2048,1536]{1,0:T(8,128)(2,1)}) %all-gather.27.cloned.1.call-update) | async-done | bytes 6291472 | tf_op jit(solution)/shard_map/all_gather | solution.py:147
  516.8 36.9 %all-gather.29.cloned.1.call-done = bf16[1536,2048]{1,0:T(8,128)(2,1)} async-done(((bf16[1536,256]{1,0:T(8,128)(2,1)}), bf16[1536,2048]{1,0:T(8,128)(2,1)}) %all-gather.29.cloned.1.call-update) | async-done | bytes 6291472 | tf_op jit(solution)/shard_map/all_gather | solution.py:148
  553.7 16.4 %multiply_convert_fusion = (bf16[1024,1536]{1,0:T(8,128)(2,1)}, bf16[1024,1536]{1,0:T(8,128)(2,1)S(1)}, bf16[1024,1536]{1,0:T(8,128)(2,1)}) fusion(f32[1024,1536]{1,0:T(8,128)} %fusion.118, f32[1024,1536]{1,0:T(8,128)} %fusion.119, bf16[1536,2048]{1,0:T(8,128)(2,1)} %all-gather.29.cloned.1.call-done, ...), kind=kOutput, calls=%fused_computation.75 | convolution fusion | flops 6467616768 | bytes 32505860 | tf_op jit(solution)/shard_map/dot_general | solution.py:52
  601.8 65.7 %reduce-scatter.16.cloned.1.call-done = bf16[256,2048]{1,0:T(8,128)(2,1)} async-done(((bf16[1024,2048]{1,0:T(8,128)(2,1)}), bf16[256,2048]{1,0:T(8,128)(2,1)}) %reduce-scatter.16.cloned.1.call-update) | async-done | bytes 1048592 | tf_op jit(solution)/shard_map/reduce_scatter | solution.py:231
  670.3 76.6 %reduce-scatter.14.cloned.1.call-done = bf16[256,2048]{1,0:T(8,128)(2,1)} async-done(((bf16[1024,2048]{1,0:T(8,128)(2,1)}), bf16[256,2048]{1,0:T(8,128)(2,1)}) %reduce-scatter.14.cloned.1.call-update) | async-done | bytes 1048592 | tf_op jit(solution)/shard_map/reduce_scatter | solution.py:192
  790.3 43.1 %all-gather.31.cloned.1.call-done = bf16[1024,2048]{1,0:T(8,128)(2,1)} async-done(((bf16[256,2048]{1,0:T(8,128)(2,1)}), bf16[1024,2048]{1,0:T(8,128)(2,1)}) %all-gather.31.cloned.1.call-update) | async-done | bytes 4194320 | tf_op jit(solution)/shard_map/all_gather | solution.py:242
  842.1 27.5 %while.29 = (s32[]{:T(128)}, f32[2,1024,2,128]{1,3,2,0:T(8,128)}, f32[2,1024,128]{2,1,0:T(8,128)}, bf16[2,1024,128]{2,1,0:T(8,128)(2,1)}, bf16[2,1024,128]{2,1,0...) while((s32[]{:T(128)}, f32[2,1024,2,128]{1,3,2,0:T(8,128)}, ...), condition=%wide.region_16.17_spmd.clone, body=%wide.region_14.16_spmd.clone.sunk | while | flops 2719348736 | bytes 101516552 | solution.py:248
  914.9 47.5 %reduce-scatter.28.cloned.1.call-done = bf16[256,1536]{1,0:T(8,128)(2,1)} async-done(((bf16[2048,1536]{1,0:T(8,128)(2,1)}), bf16[256,1536]{1,0:T(8,128)(2,1)}) %reduce-scatter.28.cloned.1.call-update) | async-done | bytes 786448 | tf_op jit(solution)/shard_map/reduce_scatter | solution.py:308
  964.8 62.9 %reduce-scatter.30.cloned.1.call-done = bf16[256,1536]{1,0:T(8,128)(2,1)} async-done(((bf16[2048,1536]{1,0:T(8,128)(2,1)}), bf16[256,1536]{1,0:T(8,128)(2,1)}) %reduce-scatter.30.cloned.1.call-update) | async-done | bytes 786448 | tf_op jit(solution)/shard_map/reduce_scatter | solution.py:311
  1030.2 36.6 %reduce-scatter.22.cloned.1.call-done = bf16[256,256]{1,0:T(8,128)(2,1)} async-done(((bf16[2048,256]{1,0:T(8,128)(2,1)}), bf16[256,256]{1,0:T(8,128)(2,1)}) %reduce-scatter.22.cloned.1.call-update) | async-done | bytes 131088 | tf_op jit(solution)/shard_map/reduce_scatter | solution.py:290
  1068.4 37.4 %reduce-scatter.24.cloned.1.call-done = bf16[256,256]{1,0:T(8,128)(2,1)} async-done(((bf16[2048,256]{1,0:T(8,128)(2,1)}), bf16[256,256]{1,0:T(8,128)(2,1)}) %reduce-scatter.24.cloned.1.call-update) | async-done | bytes 131088 | tf_op jit(solution)/shard_map/reduce_scatter | solution.py:293
  1107.5 42.9 %reduce-scatter.26.cloned.1.call-done = bf16[512,256]{1,0:T(8,128)(2,1)} async-done(((bf16[512,2048]{1,0:T(8,128)(2,1)}), bf16[512,256]{1,0:T(8,128)(2,1)}) %reduce-scatter.26.cloned.1.call-update) | async-done | bytes 262160 | tf_op jit(solution)/shard_map/reduce_scatter | solution.py:302
  1152.1 43.0 %reduce-scatter.20.cloned.1.call-done = bf16[256,512]{1,0:T(8,128)(2,1)} async-done(((bf16[2048,512]{1,0:T(8,128)(2,1)}), bf16[256,512]{1,0:T(8,128)(2,1)}) %reduce-scatter.20.cloned.1.call-update) | async-done | bytes 262160 | tf_op jit(solution)/shard_map/reduce_scatter | solution.py:287
  1196.9 77.3 %reduce-scatter.18.cloned.1.call-done = bf16[256,2048]{1,0:T(8,128)(2,1)} async-done(((bf16[1024,2048]{1,0:T(8,128)(2,1)}), bf16[256,2048]{1,0:T(8,128)(2,1)}) %reduce-scatter.18.cloned.1.call-update) | async-done | bytes 1048592 | tf_op jit(solution)/shard_map/reduce_scatter | solution.py:271
  1276.1 18.2 %all-reduce.6 = (bf16[2048]{0:T(1024)(128)(2,1)S(1)}, bf16[128]{0:T(256)(128)(2,1)S(1)}, bf16[128]{0:T(256)(128)(2,1)S(1)}, bf16[2048]{0:T(1024)(128)(2,1)S(1)}) all-reduce(f32[2048]{0:T(1024)S(1)} %get-tuple-element.175, f32[128]{0:T(128)S(1)} %bitcast_reduce_fusion, ...), channel_id=1, replica_groups=mesh['dp'=8,'tensor'=4] {'tensor'}, use_global_device_ids=true, to_apply=%region_22.23 | all-reduce | flops 4352 | bytes 26112 | tf_op jit(solution)/shard_map/psum | solution.py:281
  (316 shorter events, 346.3 us)
Async XLA Ops:
  7.2 40.4 %all-gather.15.cloned.1.call-start = ((), (), s32[]{:S(2)}) async-start(), calls=%async_computation.12 | async-start | bytes 2359296 | tf_op jit(solution)/shard_map/all_gather | solution.py:139
  8.0 58.1 %all-gather.17.cloned.1.call-start = ((), (), s32[]{:S(2)}) async-start(), calls=%async_computation.13 | async-start | bytes 1179648 | tf_op jit(solution)/shard_map/all_gather | solution.py:140
  8.7 82.8 %all-gather.19.cloned.1.call-start = ((), (), s32[]{:S(2)}) async-start(), calls=%async_computation.14 | async-start | bytes 1179648 | tf_op jit(solution)/shard_map/all_gather | solution.py:141
  9.5 164.9 %all-gather.13.cloned.1.call-start = ((), (), s32[]{:S(2)}) async-start(), calls=%async_computation.11 | async-start | bytes 5242880 | tf_op jit(solution)/shard_map/all_gather | solution.py:156
  25.7 197.4 %all-gather.21.cloned.1.call-start = ((), (), s32[]{:S(2)}) async-start(), calls=%async_computation.15 | async-start | bytes 2359296 | tf_op jit(solution)/shard_map/all_gather | solution.py:144
  26.3 279.5 %reduce-scatter.12.cloned.1.call-start = ((), (), s32[]{:S(2)}) async-start(), calls=%async_computation.16 | async-start | bytes 5242880 | tf_op jit(solution)/shard_map/reduce_scatter | solution.py:179
  230.3 199.2 %all-gather.25.cloned.1.call-start = ((), (), s32[]{:S(2)}) async-start(), calls=%async_computation.18 | async-start | bytes 7077888 | tf_op jit(solution)/shard_map/all_gather | solution.py:146
  231.1 228.1 %all-gather.23.cloned.1.call-start = ((), (), s32[]{:S(2)}) async-start(), calls=%async_computation.17 | async-start | bytes 5242880 | tf_op jit(solution)/shard_map/all_gather | solution.py:187
  310.0 195.1 %all-gather.27.cloned.1.call-start = ((), (), s32[]{:S(2)}) async-start(), calls=%async_computation.19 | async-start | bytes 7077888 | tf_op jit(solution)/shard_map/all_gather | solution.py:147
  310.7 242.9 %all-gather.29.cloned.1.call-start = ((), (), s32[]{:S(2)}) async-start(), calls=%async_computation.20 | async-start | bytes 7077888 | tf_op jit(solution)/shard_map/all_gather | solution.py:148
  311.3 356.1 %reduce-scatter.16.cloned.1.call-start = ((), (), s32[]{:S(2)}) async-start(), calls=%async_computation.22 | async-start | bytes 5242880 | tf_op jit(solution)/shard_map/reduce_scatter | solution.py:231
  312.3 26.8 %collective-permute-start = (bf16[256,2048]{1,0:T(8,128)(2,1)S(1)}, bf16[256,2048]{1,0:T(8,128)(2,1)S(1)}, u32[]{:S(2)}, u32[]{:S(2)}) collective-permute-start(bf16[256,2048]{1,0:T(8,128)(2,1)S(1)} %fusion.97), channel_id=1, source_target_pairs={{0,1},{1,2},{2,3},{3,0},{4,5},{5,6},{6,7},{7,4},{8,9},{9,10},{10,1... | collective-permute-start | bytes 3145736 | tf_op jit(solution)/shard_map/ppermute | solution.py:217
  340.0 26.0 %collective-permute-start.1 = (bf16[256,2048]{1,0:T(8,128)(2,1)S(1)}, bf16[256,2048]{1,0:T(8,128)(2,1)}, u32[]{:S(2)}, u32[]{:S(2)}) collective-permute-start(bf16[256,2048]{1,0:T(8,128)(2,1)S(1)} %collective-permute-done), channel_id=1, source_target_pairs={{0,1},{1,2},{2,3},{3,0},{4,5},{5,6},{6,7},{7,4},{8,9},{9,10},{10,1... | collective-permute-start | bytes 3145736 | tf_op jit(solution)/shard_map/ppermute | solution.py:217
  366.0 49.5 %collective-permute-start.2 = (bf16[256,2048]{1,0:T(8,128)(2,1)}, bf16[256,2048]{1,0:T(8,128)(2,1)}, u32[]{:S(2)}, u32[]{:S(2)}) collective-permute-start(bf16[256,2048]{1,0:T(8,128)(2,1)} %collective-permute-done.1), channel_id=1, source_target_pairs={{0,1},{1,2},{2,3},{3,0},{4,5},{5,6},{6,7},{7,4},{8,9},{9,10},{10,1... | collective-permute-start | bytes 3145736 | tf_op jit(solution)/shard_map/ppermute | solution.py:217
  590.5 156.4 %reduce-scatter.14.cloned.1.call-start = ((), (), s32[]{:S(2)}) async-start(), calls=%async_computation.21 | async-start | bytes 5242880 | tf_op jit(solution)/shard_map/reduce_scatter | solution.py:192
  601.7 231.7 %all-gather.31.cloned.1.call-start = ((), (), s32[]{:S(2)}) async-start(), calls=%async_computation.23 | async-start | bytes 5242880 | tf_op jit(solution)/shard_map/all_gather | solution.py:242
  752.0 160.3 %reduce-scatter.32.cloned.1.call-start = ((), (), s32[]{:S(2)}) async-start(), calls=%async_computation.31 | async-start | bytes 7077888 | tf_op jit(solution)/shard_map/reduce_scatter | solution.py:314
  763.3 199.0 %reduce-scatter.28.cloned.1.call-start = ((), (), s32[]{:S(2)}) async-start(), calls=%async_computation.29 | async-start | bytes 7077888 | tf_op jit(solution)/shard_map/reduce_scatter | solution.py:308
  775.3 252.4 %reduce-scatter.30.cloned.1.call-start = ((), (), s32[]{:S(2)}) async-start(), calls=%async_computation.30 | async-start | bytes 7077888 | tf_op jit(solution)/shard_map/reduce_scatter | solution.py:311
  790.3 276.5 %reduce-scatter.22.cloned.1.call-start = ((), (), s32[]{:S(2)}) async-start(), calls=%async_computation.26 | async-start | bytes 1179648 | tf_op jit(solution)/shard_map/reduce_scatter | solution.py:290
  892.3 213.5 %reduce-scatter.24.cloned.1.call-start = ((), (), s32[]{:S(2)}) async-start(), calls=%async_computation.27 | async-start | bytes 1179648 | tf_op jit(solution)/shard_map/reduce_scatter | solution.py:293
  892.9 257.4 %reduce-scatter.26.cloned.1.call-start = ((), (), s32[]{:S(2)}) async-start(), calls=%async_computation.28 | async-start | bytes 2359296 | tf_op jit(solution)/shard_map/reduce_scatter | solution.py:302
  899.2 295.9 %reduce-scatter.20.cloned.1.call-start = ((), (), s32[]{:S(2)}) async-start(), calls=%async_computation.25 | async-start | bytes 2359296 | tf_op jit(solution)/shard_map/reduce_scatter | solution.py:287
  902.4 371.8 %reduce-scatter.18.cloned.1.call-start = ((), (), s32[]{:S(2)}) async-start(), calls=%async_computation.24 | async-start | bytes 5242880 | tf_op jit(solution)/shard_map/reduce_scatter | solution.py:271
  (64 other events, 3058.2 us)
Sparse Core Ops, SparseCore 0:
  10.0 30.6 all-gather.14
  42.5 23.5 all-gather.16
  68.0 23.4 all-gather.18
  93.5 80.7 all-gather.12
  176.0 26.7 all-gather.20
  230.4 75.2 reduce-scatter.11
  307.8 46.0 all-gather.24
  356.0 103.0 all-gather.22
  461.2 43.8 all-gather.26
  507.0 46.6 all-gather.28
  590.7 76.7 reduce-scatter.15
  669.6 77.2 reduce-scatter.13
  752.1 81.2 all-gather.30
  837.0 60.2 reduce-scatter.31
  900.5 61.7 reduce-scatter.27
  965.9 61.7 reduce-scatter.29
  1030.7 36.0 reduce-scatter.21
  1069.8 35.9 reduce-scatter.23
  1109.1 41.1 reduce-scatter.25
  1153.8 41.2 reduce-scatter.19
  1197.4 76.7 reduce-scatter.17
